TPU v7x, 32 devices: a whole 2x2x4 slice. The times are simulated.
32 devices in a mesh: freq: 4 (over x, core), grid: 8 (over z, y).
Axes of the slice: x: 2, y: 2, z: 4, core: 2. Of those that a mesh axis runs over, the one named last changes fastest.
Arguments:
- series: bfloat16 [128, 1024, 256], P('freq', 'grid'), may hold values from -8 to 8
- bins: int32 [4], replicated, may hold values from 32 to 127
- sensor_coords: int32 [3, 1024], replicated, may hold values from 0 to 63
- grid_coords: int32 [3, 2048], P(None, 'grid'), may hold values from 0 to 63
Outputs:
- bin_power: float32 [4, 2048], P('freq', 'grid')
- power: float32 [2048], P('grid')
All inputs are finite; a program needn't handle non-finite values.
Results may differ from a plain program's by a relative error of at most 0.0015.
Values may be sent and summed in bfloat16 or wider, within the bound.
No kernel may reach another device: no remote copies, remote signals or barrier semaphores. Data moves between devices by JAX's collectives and lax.ppermute only.
A program may use at most 64 MiB of HBM per device.

v0:
```python
import math
import jax
import jax.numpy as jnp
from jax import lax
from jax.sharding import PartitionSpec as P


def on_device(series, bins, sensor_coords, grid_coords):
    snap_local, channel_local, samples = series.shape
    all_bins = bins.shape[0]
    sample_index = jnp.arange(samples, dtype=jnp.int32)
    cycles = bins[:, None] * sample_index[None, :] % samples
    angles = 2.0 * math.pi / samples * cycles.astype(jnp.float32)
    scaling = (samples / 2.0) ** (-0.5)
    transform_table = jnp.stack([jnp.cos(angles) * scaling, -jnp.sin(angles) * scaling], 1)
    transform_table = transform_table.astype(jnp.bfloat16).reshape(2 * all_bins, samples)
    spectra = jnp.einsum("kt,sct->kcs", transform_table, series, preferred_element_type=jnp.float32)
    spectra = spectra.astype(jnp.bfloat16).reshape(all_bins, 2, channel_local, snap_local)
    regrouped = lax.all_to_all(spectra, "freq", split_axis=0, concat_axis=3, tiled=True)
    bin_count = regrouped.shape[0]
    snap_total = regrouped.shape[3]
    gathered = lax.all_gather(regrouped, "grid", axis=2, tiled=True)
    channels = gathered.shape[2]
    local_bins = lax.dynamic_slice_in_dim(bins, lax.axis_index("freq") * bin_count, bin_count)
    squared = jnp.zeros((grid_coords.shape[1], channels), jnp.int32)
    for axis_pos in range(3):
        offsets = grid_coords[axis_pos][:, None] - sensor_coords[axis_pos][None, :]
        squared = squared + offsets * offsets
    distance = jnp.sqrt(squared.astype(jnp.float32))
    phases = (
        4.0 * math.pi / samples * local_bins.astype(jnp.float32)[:, None, None] * distance[None]
    )
    amplitude = channels ** (-0.5)
    beam_real = (jnp.cos(phases) * amplitude).astype(jnp.bfloat16)
    beam_imag = (-jnp.sin(phases) * amplitude).astype(jnp.bfloat16)
    spec_real = gathered[:, 0]
    spec_imag = gathered[:, 1]

    def product(left, right):
        return jnp.einsum("fgc,fcs->fgs", left, right, preferred_element_type=jnp.float32)

    out_real = product(beam_real, spec_real) + product(beam_imag, spec_imag)
    out_imag = product(beam_real, spec_imag) - product(beam_imag, spec_real)
    bin_power = jnp.sum(out_real * out_real + out_imag * out_imag, 2) / snap_total
    summed = lax.psum(jnp.sum(bin_power, 0), "freq")
    power = summed / (bin_count * lax.axis_size("freq"))
    return (bin_power, power)


def solution(mesh):
    return jax.shard_map(
        on_device,
        mesh=mesh,
        in_specs=(P("freq", "grid", None), P(), P(), P(None, "grid")),
        out_specs=(P("freq", "grid"), P("grid")),
        check_vma=False,
    )
```

profile of v0, /device:TPU:0, one launch (start us, length us, event | category | flops | bytes accessed | tf_op | source)
XLA Modules:
  0.0 64.2 jit_solution(2394044324553024529)
XLA Ops:
  0.6 0.0 copy-start
  0.6 0.0 copy-start.4
  0.7 0.0 copy-start.1
  0.7 0.0 copy-start.3
  0.7 0.9 %multiply_convert_fusion.3 = (bf16[4,1,256]{2,0,1:T(4,128)(2,1)S(1)}, bf16[4,1,256]{2,0,1:T(4,128)(2,1)S(1)}) fusion(s32[4]{0:T(128)} %param.5), kind=kLoop, calls=%fused_computation.24 | loop fusion | flops 19456 | bytes 4112 | tf_op jit(solution)/shard_map/convert
  1.6 0.6 copy-done
  2.3 0.6 convolution_convert_fusion
  2.9 0.6 %copy.12 = bf16[4,2,128,32]{2,3,1,0:T(8,128)(2,1)} copy(bf16[4,2,128,32]{2,1,0,3:T(2,128)(2,1)S(1)} %bitcast.34) | data formatting | bytes 131072 | tf_op jit(solution)/shard_map/reshape | solution.py:18
  3.6 4.2 %all-to-all-start = ((bf16[4,2,128,32]{2,3,1,0:T(8,128)(2,1)}), bf16[4,2,128,32]{2,3,1,0:T(8,128)(2,1)S(1)}, u32[]{:S(2)}, u32[]{:S(2)}) async-start(bf16[4,2,128,32]{2,3,1,0:T(8,128)(2,1)} %copy.12), calls=%async_computation | async-start | bytes 131072 | tf_op jit(solution)/shard_map/all_to_all | solution.py:19
  7.8 0.0 copy-done.1
  7.8 0.0 copy-done.3
  7.8 0.0 copy-done.4
  7.9 0.6 dynamic_slice.3
  9.1 2.8 %all-to-all-done = bf16[4,2,128,32]{2,3,1,0:T(8,128)(2,1)S(1)} async-done(((bf16[4,2,128,32]{2,3,1,0:T(8,128)(2,1)}), bf16[4,2,128,32]{2,3,1,0:T(8,128)(2,1)S(1)}, u32[]{:S(2)}, u32[]{:S(2)}) %all-to-all-start) | async-done | bytes 65568 | tf_op jit(solution)/shard_map/all_to_all | solution.py:19
  11.9 28.8 %all_gather.3 = bf16[1,2,1024,128]{2,3,1,0:T(8,128)(2,1)S(1)} all-gather(bf16[1,2,128,128]{2,3,1,0:T(8,128)(2,1)S(1)} %bitcast.35), channel_id=1, replica_groups=mesh['freq'=4,'grid'=8] {'grid'}, dimensions={2}, use_global_device_ids=true | all-gather | bytes 589824 | tf_op jit(solution)/shard_map/all_gather | solution.py:22
  40.7 4.2 %fusion.8 = f32[256,128]{0,1:T(8,128)S(1)} fusion(s32[1024]{0:T(1024)S(1)} %bitcast.41, s32[256]{0:T(256)S(1)} %bitcast.53, s32[1024]{0:T(1024)S(1)} %bitcast.45, s32[256]{0:T(256)S(1)} %bitcast.57, s32[1024]{0:T(1024)S(1)} %bitcast.37, s32[256]{0:T(256)S(1)} %bitcast.49, f32[]{:T(128)} %bitcast, bf16[1,2,1024,128]{2,3,1,0:T(8,128)(2,1)S(1)} %all_gather.3), kind=kOutput, calls=%fused_computation.12 | convolution fusion | flops 70254592 | bytes 408580 | tf_op jit(solution)/shard_map/fgc,fcs->fgs/dot_general | solution.py:40
  44.9 4.2 %fusion.10 = f32[256,128]{0,1:T(8,128)S(1)} fusion(s32[1024]{0:T(1024)S(1)} %bitcast.42, s32[256]{0:T(256)S(1)} %bitcast.54, s32[1024]{0:T(1024)S(1)} %bitcast.46, s32[256]{0:T(256)S(1)} %bitcast.58, s32[1024]{0:T(1024)S(1)} %bitcast.38, s32[256]{0:T(256)S(1)} %bitcast.50, f32[]{:T(128)} %bitcast, bf16[1,2,1024,128]{2,3,1,0:T(8,128)(2,1)S(1)} %all_gather.3), kind=kOutput, calls=%fused_computation.13 | convolution fusion | flops 70254592 | bytes 408580 | tf_op jit(solution)/shard_map/fgc,fcs->fgs/dot_general | solution.py:40
  49.1 4.4 %fusion.2 = f32[256,128]{0,1:T(8,128)S(1)} fusion(f32[256,128]{0,1:T(8,128)S(1)} %fusion.10, s32[1024]{0:T(1024)S(1)} %bitcast.43, s32[256]{0:T(256)S(1)} %bitcast.55, s32[1024]{0:T(1024)S(1)} %bitcast.47, s32[256]{0:T(256)S(1)} %bitcast.59, s32[1024]{0:T(1024)S(1)} %bitcast.39, s32[256]{0:T(256)S(1)} %bitcast.51, f32[]{:T(128)} %bitcast, ...), kind=kOutput, calls=%fused_computation.4 | convolution fusion | flops 70582272 | bytes 539652 | tf_op jit(solution)/shard_map/fgc,fcs->fgs/dot_general | solution.py:40
  53.6 4.3 %fusion.3 = f32[256]{0:T(256)S(1)} fusion(f32[256,128]{0,1:T(8,128)S(1)} %fusion.2, f32[256,128]{0,1:T(8,128)S(1)} %fusion.8, s32[1024]{0:T(1024)S(1)} %bitcast.44, s32[256]{0:T(256)S(1)} %bitcast.56, s32[1024]{0:T(1024)S(1)} %bitcast.48, s32[256]{0:T(256)S(1)} %bitcast.60, s32[1024]{0:T(1024)S(1)} %bitcast.40, s32[256]{0:T(256)S(1)} %bitcast.52, f32[]{:T(128)} %bitcast, ...), kind=kOutput, calls=%fused_computation.6 | convolution fusion | flops 70647552 | bytes 540676 | tf_op jit(solution)/shard_map/fgc,fcs->fgs/dot_general | solution.py:40
  57.8 0.0 copy-start.2
  57.9 5.8 %psum.7 = f32[256]{0:T(256)S(1)} all-reduce(f32[256]{0:T(256)S(1)} %broadcast_multiply_fusion.1), channel_id=1, replica_groups=mesh['freq'=4,'grid'=8] {'freq'}, use_global_device_ids=true, to_apply=%region_1.2 | all-reduce | flops 256 | bytes 2048 | tf_op jit(solution)/shard_map/psum | solution.py:45
  63.6 0.6 broadcast_multiply_fusion
  64.2 0.0 copy-done.2
  (7 shorter events, 0.1 us)
Async XLA Ops:
  0.6 1.6 %copy-start = (bf16[32,128,256]{2,1,0:T(8,128)(2,1)S(1)}, bf16[32,128,256]{2,1,0:T(8,128)(2,1)}, u32[]{:S(2)}) copy-start(bf16[32,128,256]{2,1,0:T(8,128)(2,1)} %param.4) | copy-start | bytes 6291460
  0.6 7.2 %copy-start.4 = (s32[4]{0:T(128)S(1)}, s32[4]{0:T(128)}, u32[]{:S(2)}) copy-start(s32[4]{0:T(128)} %param.5) | copy-start | bytes 52
  0.7 7.1 %copy-start.1 = (s32[3,1024]{1,0:T(4,128)S(1)}, s32[3,1024]{1,0:T(4,128)}, u32[]{:S(2)}) copy-start(s32[3,1024]{1,0:T(4,128)} %param.6) | copy-start | bytes 36868
  0.7 7.2 %copy-start.3 = (s32[3,256]{1,0:T(4,128)S(1)}, s32[3,256]{1,0:T(4,128)}, u32[]{:S(2)}) copy-start(s32[3,256]{1,0:T(4,128)} %param.7) | copy-start | bytes 9220
  3.6 8.4 %all-to-all-start = ((bf16[4,2,128,32]{2,3,1,0:T(8,128)(2,1)}), bf16[4,2,128,32]{2,3,1,0:T(8,128)(2,1)S(1)}, u32[]{:S(2)}, u32[]{:S(2)}) async-start(bf16[4,2,128,32]{2,3,1,0:T(8,128)(2,1)} %copy.12), calls=%async_computation | async-start | bytes 131072 | tf_op jit(solution)/shard_map/all_to_all | solution.py:19
  57.8 6.3 %copy-start.2 = (f32[256]{0:T(256)}, f32[256]{0:T(256)S(1)}, u32[]{:S(2)}) copy-start(f32[256]{0:T(256)S(1)} %broadcast_multiply_fusion.1) | copy-start | bytes 3076
where the time goes:
time: 64.5 us; the launch traced here: 64.2 us
  blocking collectives  34.5 us (53%)
  matrix products  17.7 us (27%)
  starting transfers between devices  4.24 us (7%)
  waiting for transfers between devices  2.83 us (4%)
  local copies, waits for them, and re-layouts  1.93 us (3%)
  other arithmetic  1.51 us (2%)
  between operations  1.41 us (2%)
    all_gather x1, blocking collectives, on_device(): gathered = lax.all_gather(regrouped, 'grid', axis=2, tiled=True)  28.8 us
    dot_general x4, matrix products, product(): jnp.einsum('fgc,fcs->fgs', left, right, preferred_element_type=jnp.float32)  17.1 us
    psum x1, blocking collectives, on_device(): summed = lax.psum(jnp.sum(bin_power, 0), 'freq')  5.76 us
    all_to_all x1, starting transfers between devices, on_device(): lax.all_to_all(spectra, 'freq', split_axis=0, concat_axis=3, tiled=True)  4.24 us
    all_to_all x1, waiting for transfers between devices, on_device(): lax.all_to_all(spectra, 'freq', split_axis=0, concat_axis=3, tiled=True)  2.83 us
  transfers between devices with their start and end apart: 1, of which 1 were waited for; matrix products, arithmetic and copies ran while one was open for 1% of the time, Pallas kernels for 0%

commit v1 on v0

--- a/solution.py
+++ b/solution.py
@@ -19,7 +19,24 @@
     regrouped = lax.all_to_all(spectra, "freq", split_axis=0, concat_axis=3, tiled=True)
     bin_count = regrouped.shape[0]
     snap_total = regrouped.shape[3]
-    gathered = lax.all_gather(regrouped, "grid", axis=2, tiled=True)
+    even = jax.lax.axis_size("grid")
+    piece_out = jax.lax.axis_index("grid")
+    s_next, e_next, a_next = (even, piece_out, regrouped.shape[2])
+    known, state_now = (regrouped, 1)
+    while state_now < s_next:
+        known = jnp.concatenate(
+            [
+                known,
+                jax.lax.ppermute(
+                    known,
+                    axis_name="grid",
+                    perm=[(dev_j, (dev_j - state_now) % s_next) for dev_j in range(s_next)],
+                ),
+            ],
+            2,
+        )
+        state_now = 2 * state_now
+    gathered = jnp.roll(known, e_next * a_next, axis=2)
     channels = gathered.shape[2]
     local_bins = lax.dynamic_slice_in_dim(bins, lax.axis_index("freq") * bin_count, bin_count)
     squared = jnp.zeros((grid_coords.shape[1], channels), jnp.int32)

time: 64.5 us -> 59.1 us (0.916)
  blocking collectives: 34.5 us -> 13.9 us
  waiting for transfers between devices: 2.83 us -> 16.1 us
  starting transfers between devices: 4.24 us -> 6.47 us
    all_gather x1 -> x0, blocking collectives: 28.8 us -> none  [on_device(): gathered = lax.all_gather(regrouped, 'grid', axis=2, tiled=True)]
    ppermute x0 -> x3, waiting for transfers between devices: none -> 16.1 us  [on_device(): jax.lax.ppermute(known, axis_name='grid', perm=[(dev_j, (dev_j - state_no...]
    all_to_all x0 -> x1, blocking collectives: none -> 8.16 us  [on_device(): lax.all_to_all(spectra, 'freq', split_axis=0, concat_axis=3, tiled=True)]
    ppermute x0 -> x3, starting transfers between devices: none -> 6.47 us  [on_device(): jax.lax.ppermute(known, axis_name='grid', perm=[(dev_j, (dev_j - state_no...]
    all_to_all x1 -> x0, starting transfers between devices: 4.24 us -> none  [on_device(): lax.all_to_all(spectra, 'freq', split_axis=0, concat_axis=3, tiled=True)]
    all_to_all x1 -> x0, waiting for transfers between devices: 2.83 us -> none  [on_device(): lax.all_to_all(spectra, 'freq', split_axis=0, concat_axis=3, tiled=True)]
  transfers between devices with their start and end apart: 1 -> 3, of which waited for: 1 -> 3; matrix products, arithmetic and copies ran while one was open for 1% -> 1% of each run, Pallas kernels for 0% -> 0%
where the time goes in v1:
time: 59.1 us; the launch traced here: 58.7 us
  matrix products  17.7 us (30%)
  waiting for transfers between devices  16.1 us (27%)
  blocking collectives  13.9 us (24%)
  starting transfers between devices  6.47 us (11%)
  other arithmetic  1.55 us (3%)
  between operations  1.49 us (3%)
  local copies, waits for them, and re-layouts  1.43 us (2%)
    dot_general x4, matrix products, product(): jnp.einsum('fgc,fcs->fgs', left, right, preferred_element_type=jnp.float32)  17.1 us
    ppermute x3, waiting for transfers between devices, on_device(): jax.lax.ppermute(known, axis_name='grid', perm=[(dev_j, (dev_j - state_no...  16.1 us
    all_to_all x1, blocking collectives, on_device(): lax.all_to_all(spectra, 'freq', split_axis=0, concat_axis=3, tiled=True)  8.16 us
    ppermute x3, starting transfers between devices, on_device(): jax.lax.ppermute(known, axis_name='grid', perm=[(dev_j, (dev_j - state_no...  6.47 us
    psum x1, blocking collectives, on_device(): summed = lax.psum(jnp.sum(bin_power, 0), 'freq')  5.76 us
  transfers between devices with their start and end apart: 3, of which 3 were waited for; matrix products, arithmetic and copies ran while one was open for 1% of the time, Pallas kernels for 0%

profile of v1, /device:TPU:0, one launch (start us, length us, event | category | flops | bytes accessed | tf_op | source)
XLA Modules:
  0.0 58.7 jit_solution(15893372353346681737)
XLA Ops:
  0.6 0.0 copy-start
  0.6 0.0 copy-start.4
  0.7 0.0 copy-start.1
  0.7 0.0 copy-start.3
  0.7 0.9 %multiply_convert_fusion.3 = (bf16[4,1,256]{2,0,1:T(4,128)(2,1)S(1)}, bf16[4,1,256]{2,0,1:T(4,128)(2,1)S(1)}) fusion(s32[4]{0:T(128)} %param.5), kind=kLoop, calls=%fused_computation.34 | loop fusion | flops 19456 | bytes 4112 | tf_op jit(solution)/shard_map/convert
  1.6 0.6 %copy-done = bf16[32,128,256]{2,1,0:T(8,128)(2,1)S(1)} copy-done((bf16[32,128,256]{2,1,0:T(8,128)(2,1)S(1)}, bf16[32,128,256]{2,1,0:T(8,128)(2,1)}, u32[]{:S(2)}) %copy-start) | copy-done | bytes 2097176
  2.3 0.6 %convolution_convert_fusion = bf16[8,32,128]{2,0,1:T(8,128)(2,1)S(1)} fusion(bf16[8,256,1]{1,0,2:T(8,128)(2,1)S(1)} %reshape.730, bf16[32,128,256]{2,1,0:T(8,128)(2,1)S(1)} %copy-done), kind=kOutput, calls=%fused_computation.5 | convolution fusion | flops 16809984 | bytes 2166784 | tf_op jit(solution)/shard_map/kt,sct->kcs/dot_general | solution.py:17
  2.9 8.2 %all_to_all.18 = bf16[4,2,128,32]{2,3,1,0:T(8,128)(2,1)S(1)} all-to-all(bf16[4,2,128,32]{2,3,1,0:T(8,128)(2,1)S(1)} %copy.12), channel_id=1, replica_groups=mesh['freq'=4,'grid'=8] {'freq'}, dimensions={0} | all-to-all | bytes 131072 | tf_op jit(solution)/shard_map/all_to_all | solution.py:19
  11.1 4.6 %collective-permute-start = (bf16[1,2,128,128]{2,3,1,0:T(8,128)(2,1)S(1)}, bf16[1,2,128,128]{2,3,1,0:T(8,128)(2,1)S(1)}, u32[]{:S(2)}, u32[]{:S(2)}) collective-permute-start(bf16[1,2,128,128]{2,3,1,0:T(8,128)(2,1)S(1)} %bitcast.34), channel_id=1, source_target_pairs={{0,7},{1,0},{2,1},{3,2},{4,3},{5,4},{6,5},{7,6},{8,15},{9,8},{10,9... | collective-permute-start | bytes 196616 | tf_op jit(solution)/shard_map/ppermute | solution.py:30
  15.7 0.0 copy-done.1
  15.7 0.0 copy-done.4
  15.7 0.6 dynamic_slice.7
  16.9 0.6 %collective-permute-done = bf16[1,2,128,128]{2,3,1,0:T(8,128)(2,1)S(1)} collective-permute-done((bf16[1,2,128,128]{2,3,1,0:T(8,128)(2,1)S(1)}, bf16[1,2,128,128]{2,3,1,0:T(8,128)(2,1)S(1)}, u32[]{:S(2)}, u32[]{:S(2)}) %collective-permute-start) | collective-permute-done | bytes 65568 | tf_op jit(solution)/shard_map/ppermute | solution.py:30
  17.6 1.5 %collective-permute-start.1 = (bf16[1,2,256,128]{2,3,1,0:T(8,128)(2,1)S(1)}, bf16[1,2,256,128]{2,3,1,0:T(8,128)(2,1)S(1)}, u32[]{:S(2)}, u32[]{:S(2)}) collective-permute-start(bf16[1,2,256,128]{2,3,1,0:T(8,128)(2,1)S(1)} %pad_maximum_fusion.1), channel_id=1, source_target_pairs={{0,6},{1,7},{2,0},{3,1},{4,2},{5,3},{6,4},{7,5},{8,14},{9,15},{10,... | collective-permute-start | bytes 393224 | tf_op jit(solution)/shard_map/ppermute | solution.py:30
  19.0 3.6 %collective-permute-done.1 = bf16[1,2,256,128]{2,3,1,0:T(8,128)(2,1)S(1)} collective-permute-done((bf16[1,2,256,128]{2,3,1,0:T(8,128)(2,1)S(1)}, bf16[1,2,256,128]{2,3,1,0:T(8,128)(2,1)S(1)}, u32[]{:S(2)}, u32[]{:S(2)}) %collective-permute-start.1) | collective-permute-done | bytes 131104 | tf_op jit(solution)/shard_map/ppermute | solution.py:30
  22.6 0.5 collective-permute-start.2
  23.1 11.9 %collective-permute-done.2 = bf16[1,2,512,128]{2,3,1,0:T(8,128)(2,1)S(1)} collective-permute-done((bf16[1,2,512,128]{2,3,1,0:T(8,128)(2,1)S(1)}, bf16[1,2,512,128]{2,3,1,0:T(8,128)(2,1)S(1)}, u32[]{:S(2)}, u32[]{:S(2)}) %collective-permute-start.2) | collective-permute-done | bytes 262176 | tf_op jit(solution)/shard_map/ppermute | solution.py:30
  35.2 4.2 %fusion.8 = f32[256,128]{0,1:T(8,128)S(1)} fusion(s32[1024]{0:T(1024)S(1)} %bitcast.45, s32[256]{0:T(256)S(1)} %bitcast.57, s32[1024]{0:T(1024)S(1)} %bitcast.49, s32[256]{0:T(256)S(1)} %bitcast.61, s32[1024]{0:T(1024)S(1)} %bitcast.41, s32[256]{0:T(256)S(1)} %bitcast.53, f32[]{:T(128)} %bitcast, ...), kind=kOutput, calls=%fused_computation.12 | convolution fusion | flops 70516736 | bytes 408584 | tf_op jit(solution)/shard_map/fgc,fcs->fgs/dot_general | solution.py:57
  39.5 4.2 %fusion.10 = f32[256,128]{0,1:T(8,128)S(1)} fusion(s32[1024]{0:T(1024)S(1)} %bitcast.46, s32[256]{0:T(256)S(1)} %bitcast.58, s32[1024]{0:T(1024)S(1)} %bitcast.50, s32[256]{0:T(256)S(1)} %bitcast.62, s32[1024]{0:T(1024)S(1)} %bitcast.42, s32[256]{0:T(256)S(1)} %bitcast.54, f32[]{:T(128)} %bitcast, ...), kind=kOutput, calls=%fused_computation.13 | convolution fusion | flops 70516736 | bytes 408588 | tf_op jit(solution)/shard_map/fgc,fcs->fgs/dot_general | solution.py:57
  43.7 4.4 %fusion.2 = f32[256,128]{0,1:T(8,128)S(1)} fusion(f32[256,128]{0,1:T(8,128)S(1)} %fusion.10, s32[1024]{0:T(1024)S(1)} %bitcast.47, s32[256]{0:T(256)S(1)} %bitcast.59, s32[1024]{0:T(1024)S(1)} %bitcast.51, s32[256]{0:T(256)S(1)} %bitcast.63, s32[1024]{0:T(1024)S(1)} %bitcast.43, s32[256]{0:T(256)S(1)} %bitcast.55, f32[]{:T(128)} %bitcast, ...), kind=kOutput, calls=%fused_computation.4 | convolution fusion | flops 70320128 | bytes 539656 | tf_op jit(solution)/shard_map/fgc,fcs->fgs/dot_general | solution.py:57
  48.1 4.2 %fusion.3 = f32[256]{0:T(256)S(1)} fusion(f32[256,128]{0,1:T(8,128)S(1)} %fusion.2, f32[256,128]{0,1:T(8,128)S(1)} %fusion.8, s32[1024]{0:T(1024)S(1)} %bitcast.48, s32[256]{0:T(256)S(1)} %bitcast.60, s32[1024]{0:T(1024)S(1)} %bitcast.52, s32[256]{0:T(256)S(1)} %bitcast.64, s32[1024]{0:T(1024)S(1)} %bitcast.44, s32[256]{0:T(256)S(1)} %bitcast.56, f32[]{:T(128)} %bitcast, ...), kind=kOutput, calls=%fused_computation.6 | convolution fusion | flops 70385408 | bytes 540684 | tf_op jit(solution)/shard_map/fgc,fcs->fgs/dot_general | solution.py:57
  52.3 0.0 copy-start.2
  52.4 5.8 %psum.7 = f32[256]{0:T(256)S(1)} all-reduce(f32[256]{0:T(256)S(1)} %broadcast_multiply_fusion.1), channel_id=1, replica_groups=mesh['freq'=4,'grid'=8] {'freq'}, use_global_device_ids=true, to_apply=%region_1.2 | all-reduce | flops 256 | bytes 2048 | tf_op jit(solution)/shard_map/psum | solution.py:62
  58.1 0.6 broadcast_multiply_fusion
  (20 shorter events, 0.3 us)
Async XLA Ops:
  0.6 1.6 %copy-start = (bf16[32,128,256]{2,1,0:T(8,128)(2,1)S(1)}, bf16[32,128,256]{2,1,0:T(8,128)(2,1)}, u32[]{:S(2)}) copy-start(bf16[32,128,256]{2,1,0:T(8,128)(2,1)} %param.4) | copy-start | bytes 6291460
  0.6 15.0 %copy-start.4 = (s32[4]{0:T(128)S(1)}, s32[4]{0:T(128)}, u32[]{:S(2)}) copy-start(s32[4]{0:T(128)} %param.5) | copy-start | bytes 52
  0.7 15.0 %copy-start.1 = (s32[3,1024]{1,0:T(4,128)S(1)}, s32[3,1024]{1,0:T(4,128)}, u32[]{:S(2)}) copy-start(s32[3,1024]{1,0:T(4,128)} %param.6) | copy-start | bytes 36868
  0.7 18.4 %copy-start.3 = (s32[3,256]{1,0:T(4,128)S(1)}, s32[3,256]{1,0:T(4,128)}, u32[]{:S(2)}) copy-start(s32[3,256]{1,0:T(4,128)} %param.7) | copy-start | bytes 9220
  11.1 6.5 %collective-permute-start = (bf16[1,2,128,128]{2,3,1,0:T(8,128)(2,1)S(1)}, bf16[1,2,128,128]{2,3,1,0:T(8,128)(2,1)S(1)}, u32[]{:S(2)}, u32[]{:S(2)}) collective-permute-start(bf16[1,2,128,128]{2,3,1,0:T(8,128)(2,1)S(1)} %bitcast.34), channel_id=1, source_target_pairs={{0,7},{1,0},{2,1},{3,2},{4,3},{5,4},{6,5},{7,6},{8,15},{9,8},{10,9... | collective-permute-start | bytes 196616 | tf_op jit(solution)/shard_map/ppermute | solution.py:30
  17.6 5.0 %collective-permute-start.1 = (bf16[1,2,256,128]{2,3,1,0:T(8,128)(2,1)S(1)}, bf16[1,2,256,128]{2,3,1,0:T(8,128)(2,1)S(1)}, u32[]{:S(2)}, u32[]{:S(2)}) collective-permute-start(bf16[1,2,256,128]{2,3,1,0:T(8,128)(2,1)S(1)} %pad_maximum_fusion.1), channel_id=1, source_target_pairs={{0,6},{1,7},{2,0},{3,1},{4,2},{5,3},{6,4},{7,5},{8,14},{9,15},{10,... | collective-permute-start | bytes 393224 | tf_op jit(solution)/shard_map/ppermute | solution.py:30
  22.6 12.4 %collective-permute-start.2 = (bf16[1,2,512,128]{2,3,1,0:T(8,128)(2,1)S(1)}, bf16[1,2,512,128]{2,3,1,0:T(8,128)(2,1)S(1)}, u32[]{:S(2)}, u32[]{:S(2)}) collective-permute-start(bf16[1,2,512,128]{2,3,1,0:T(8,128)(2,1)S(1)} %pad_maximum_fusion), channel_id=1, source_target_pairs={{0,4},{1,5},{2,6},{3,7},{4,0},{5,1},{6,2},{7,3},{8,12},{9,13},{10,... | collective-permute-start | bytes 786440 | tf_op jit(solution)/shard_map/ppermute | solution.py:30
  52.3 6.3 %copy-start.2 = (f32[256]{0:T(256)}, f32[256]{0:T(256)S(1)}, u32[]{:S(2)}) copy-start(f32[256]{0:T(256)S(1)} %broadcast_multiply_fusion.1) | copy-start | bytes 3076
